TPU v7x, 512 devices: a whole 4x4x16 slice. The times are simulated.
512 devices in a mesh: prow: 32 (over z, core), pcol: 16 (over x, y).
Axes of the slice: x: 4, y: 4, z: 16, core: 2. Of those that a mesh axis runs over, the one named last changes fastest.
Arguments:
- factor_t: bfloat16 [4, 256, 131072], P(None, 'pcol', 'prow'), may hold values from -0.03125 to 0.03125
- pattern: int32 [512, 4], P('prow'), may hold values from 0 to 1, as said below
- diag_inverse: bfloat16 [4, 256, 256], P(None, 'pcol'), as said below
- right_side: bfloat16 [131072, 256], P(('prow', 'pcol')), may hold values from -6 to 6
- later_solution: bfloat16 [131072, 256], P(('prow', 'pcol')), may hold values from -6 to 6
Outputs:
- solution: bfloat16 [4, 256, 256], P(None, 'pcol')
- reduced: bfloat16 [131072, 256], P(('prow', 'pcol'))
Inputs may be any that keep to these rules, and one draw needn't show every extreme that they name: Block row p * 16 holds the diagonal block of panel p for p < 4; its pattern is 1 exactly for the panels before p. Each diag_inverse[p] is lower triangular with a nonzero diagonal.
All inputs are finite; a program needn't handle non-finite values.
Results may differ from a plain program's by a relative error of at most 0.0047.
Values may be sent and summed in bfloat16 or wider, within the bound.
A program may use at most 64 MiB of HBM per device.

v0:
```python
import jax
import jax.numpy as jnp
from jax import lax
from jax.sharding import PartitionSpec as P


def from_root(block, axis, source):
    block = jnp.where(lax.axis_index(axis) == source, block, jnp.zeros_like(block))
    return lax.psum(block, axis)


def contract_first(left_side, right_part):
    return lax.dot_general(
        left_side, right_part, (((0,), (0,)), ((), ())), preferred_element_type=jnp.float32
    )


def on_device(factor_t, pattern, diag_inverse, right_side, later_solution):
    panels, narrow, local_rows = factor_t.shape
    width = diag_inverse.shape[2]
    columns = right_side.shape[1]
    per_device = right_side.shape[0]
    blocks = local_rows // width
    row_rank = lax.axis_index("prow")
    col_rank = lax.axis_index("pcol")
    present = jnp.broadcast_to(
        pattern.T.astype(jnp.bfloat16)[:, :, None], (panels, blocks, width)
    ).reshape(panels, local_rows)
    factor = factor_t * present[:, None, :]
    leading = factor[:, :, :width]
    counted = min(per_device, width)
    inside = col_rank * per_device < width
    top_rows = jnp.where(
        inside, right_side.astype(jnp.float32), jnp.zeros((counted, columns), jnp.float32)
    )
    strips = []
    running = top_rows
    for panel_id in range(panels):
        if panel_id > 0:
            running = running - contract_first(leading[panel_id - 1], strips[panel_id - 1])
        residual = lax.psum(running, "pcol")
        solved = jnp.dot(
            diag_inverse[panel_id],
            residual.astype(jnp.bfloat16),
            preferred_element_type=jnp.float32,
        ).astype(jnp.bfloat16)
        strips.append(from_root(solved, "prow", panel_id))
    stacked = jnp.stack(strips)
    segment = factor
    lower = lax.psum_scatter(
        lax.dot_general(
            segment, stacked, (((0, 1), (0, 1)), ((), ())), preferred_element_type=jnp.float32
        ),
        "pcol",
        scatter_dimension=0,
        tiled=True,
    )
    segment_rows = lax.all_gather(later_solution, "pcol", axis=0, tiled=True)
    count = segment_rows.shape[0]
    position = lax.iota(jnp.int32, count)
    usable = (position >= width) | (row_rank >= panels)
    cleaned = jnp.where(usable[:, None], segment_rows, jnp.zeros_like(segment_rows))
    segment = factor
    partial_bulk = lax.dot_general(
        segment, cleaned, (((2,), (0,)), ((), ())), preferred_element_type=jnp.float32
    )
    reduced = (right_side.astype(jnp.float32) - lower).astype(jnp.bfloat16)
    inverse_full = diag_inverse.astype(jnp.float32)
    own_block = jnp.zeros((width, columns), jnp.bfloat16)
    answers = [None] * panels
    for panel_id in reversed(range(panels)):
        term = partial_bulk[panel_id] + jnp.dot(
            leading[panel_id], own_block, preferred_element_type=jnp.float32
        )
        column_total = lax.psum(term, "prow")
        gap_value = stacked[panel_id].astype(jnp.float32) - column_total
        applied = lax.dot_general(
            inverse_full[panel_id],
            gap_value,
            (((0,), (0,)), ((), ())),
            precision=lax.Precision.HIGHEST,
        )
        combined = lax.psum(applied, "pcol")
        solved = combined.astype(jnp.bfloat16)
        answers[panel_id] = lax.dynamic_slice_in_dim(solved, col_rank * narrow, narrow, 0)
        own_block = jnp.where(row_rank == panel_id, solved, own_block)
    return (jnp.stack(answers), reduced)


def solution(mesh):
    in_specs = (
        P(None, "pcol", "prow"),
        P("prow", None),
        P(None, "pcol", None),
        P(("prow", "pcol"), None),
        P(("prow", "pcol"), None),
    )
    out_specs = (P(None, "pcol", None), P(("prow", "pcol"), None))
    return jax.shard_map(
        on_device, mesh=mesh, in_specs=in_specs, out_specs=out_specs, check_vma=False
    )
```

profile of v0, /device:TPU:1, one launch (start us, length us, event | category | flops | bytes accessed | tf_op | source)
XLA Modules:
  0.0 1157.3 jit_solution(9275908231909605895)
XLA Ops:
  7.2 0.7 all-gather.2.cloned.1.call-update
  8.0 0.7 convert_bitcast_fusion
  8.7 0.1 broadcast_bitcast_fusion
  8.8 0.9 convert_select_fusion
  9.7 64.1 %all-reduce.8 = bf16[256,256]{1,0:T(8,128)(2,1)S(1)} all-reduce(f32[256,256]{1,0:T(8,128)S(1)} %convert_select_fusion), channel_id=1, replica_groups=mesh['prow'=32,'pcol'=16] {'pcol'}, use_global_device_ids=true, to_apply=%region_0.1 | all-reduce | flops 65536 | bytes 393216 | tf_op jit(solution)/shard_map/psum | solution.py:41
  73.8 0.9 fusion.5
  74.6 68.3 %psum.113 = bf16[16,256]{1,0:T(8,128)(2,1)S(1)} all-reduce(bf16[16,256]{1,0:T(8,128)(2,1)S(1)} %fusion.5), channel_id=1, replica_groups=mesh['prow'=32,'pcol'=16] {'prow'}, use_global_device_ids=true, to_apply=%region_1.2 | all-reduce | flops 4096 | bytes 16384 | tf_op jit(solution)/shard_map/psum | solution.py:9
  142.9 1.1 broadcast_multiply_fusion
  144.0 0.2 convolution_subtract_fusion.2
  144.3 57.9 %all-reduce.9 = bf16[256,256]{1,0:T(8,128)(2,1)S(1)} all-reduce(f32[256,256]{1,0:T(8,128)S(1)} %convolution_subtract_fusion.2), channel_id=1, replica_groups=mesh['prow'=32,'pcol'=16] {'pcol'}, use_global_device_ids=true, to_apply=%region_2.3 | all-reduce | flops 65536 | bytes 393216 | tf_op jit(solution)/shard_map/psum | solution.py:41
  202.2 0.1 fusion.7
  202.3 60.4 %psum.115 = bf16[16,256]{1,0:T(8,128)(2,1)S(1)} all-reduce(bf16[16,256]{1,0:T(8,128)(2,1)S(1)} %fusion.7), channel_id=1, replica_groups=mesh['prow'=32,'pcol'=16] {'prow'}, use_global_device_ids=true, to_apply=%region_3.4 | all-reduce | flops 4096 | bytes 16384 | tf_op jit(solution)/shard_map/psum | solution.py:9
  262.7 0.2 convolution_subtract_fusion.1
  262.9 59.4 %all-reduce.10 = bf16[256,256]{1,0:T(8,128)(2,1)S(1)} all-reduce(f32[256,256]{1,0:T(8,128)S(1)} %convolution_subtract_fusion.1), channel_id=1, replica_groups=mesh['prow'=32,'pcol'=16] {'pcol'}, use_global_device_ids=true, to_apply=%region_4.5 | all-reduce | flops 65536 | bytes 393216 | tf_op jit(solution)/shard_map/psum | solution.py:41
  322.3 0.1 fusion.9
  322.5 61.2 %psum.117 = bf16[16,256]{1,0:T(8,128)(2,1)S(1)} all-reduce(bf16[16,256]{1,0:T(8,128)(2,1)S(1)} %fusion.9), channel_id=1, replica_groups=mesh['prow'=32,'pcol'=16] {'prow'}, use_global_device_ids=true, to_apply=%region_5.6 | all-reduce | flops 4096 | bytes 16384 | tf_op jit(solution)/shard_map/psum | solution.py:9
  383.7 0.2 convolution_subtract_fusion
  383.9 58.5 %all-reduce.11 = bf16[256,256]{1,0:T(8,128)(2,1)S(1)} all-reduce(f32[256,256]{1,0:T(8,128)S(1)} %convolution_subtract_fusion), channel_id=1, replica_groups=mesh['prow'=32,'pcol'=16] {'pcol'}, use_global_device_ids=true, to_apply=%region_6.7 | all-reduce | flops 65536 | bytes 393216 | tf_op jit(solution)/shard_map/psum | solution.py:41
  442.4 0.1 fusion.11
  442.5 60.3 %psum.119 = bf16[16,256]{1,0:T(8,128)(2,1)S(1)} all-reduce(bf16[16,256]{1,0:T(8,128)(2,1)S(1)} %fusion.11), channel_id=1, replica_groups=mesh['prow'=32,'pcol'=16] {'prow'}, use_global_device_ids=true, to_apply=%region_7.8 | all-reduce | flops 4096 | bytes 16384 | tf_op jit(solution)/shard_map/psum | solution.py:9
  502.9 2.7 convolution_bitcast_fusion
  505.6 2.3 fusion
  507.9 0.1 convolution_add_fusion.3
  508.0 89.7 %psum.120 = f32[16,256]{1,0:T(8,128)S(1)} all-reduce(f32[16,256]{1,0:T(8,128)S(1)} %convolution_add_fusion.3), channel_id=1, replica_groups=mesh['prow'=32,'pcol'=16] {'prow'}, use_global_device_ids=true, to_apply=%region_8.9 | all-reduce | flops 4096 | bytes 32768 | tf_op jit(solution)/shard_map/psum | solution.py:75
  597.7 0.3 convolution_bitcast_fusion.4
  598.0 60.2 %all-reduce.12 = bf16[256,256]{0,1:T(8,128)(2,1)S(1)} all-reduce(f32[256,256]{0,1:T(8,128)S(1)} %convolution_bitcast_fusion.4), channel_id=1, replica_groups=mesh['prow'=32,'pcol'=16] {'pcol'}, use_global_device_ids=true, to_apply=%region_9.10 | all-reduce | flops 65536 | bytes 393216 | tf_op jit(solution)/shard_map/psum | solution.py:83
  658.2 0.1 constant_dynamic-slice_fusion
  658.3 0.1 copy.10
  658.4 0.2 convolution_add_fusion.2
  658.5 103.5 %psum.122 = f32[16,256]{1,0:T(8,128)S(1)} all-reduce(f32[16,256]{1,0:T(8,128)S(1)} %convolution_add_fusion.2), channel_id=1, replica_groups=mesh['prow'=32,'pcol'=16] {'prow'}, use_global_device_ids=true, to_apply=%region_10.11 | all-reduce | flops 4096 | bytes 32768 | tf_op jit(solution)/shard_map/psum | solution.py:75
  762.1 0.3 convolution_bitcast_fusion.3
  762.4 58.6 %all-reduce.13 = bf16[256,256]{0,1:T(8,128)(2,1)S(1)} all-reduce(f32[256,256]{0,1:T(8,128)S(1)} %convolution_bitcast_fusion.3), channel_id=1, replica_groups=mesh['prow'=32,'pcol'=16] {'pcol'}, use_global_device_ids=true, to_apply=%region_11.12 | all-reduce | flops 65536 | bytes 393216 | tf_op jit(solution)/shard_map/psum | solution.py:83
  821.0 0.1 constant_dynamic-slice_fusion.1
  821.1 0.1 copy.9
  821.1 0.2 convolution_add_fusion.1
  821.3 103.3 %psum.124 = f32[16,256]{1,0:T(8,128)S(1)} all-reduce(f32[16,256]{1,0:T(8,128)S(1)} %convolution_add_fusion.1), channel_id=1, replica_groups=mesh['prow'=32,'pcol'=16] {'prow'}, use_global_device_ids=true, to_apply=%region_12.13 | all-reduce | flops 4096 | bytes 32768 | tf_op jit(solution)/shard_map/psum | solution.py:75
  924.6 0.3 convolution_bitcast_fusion.2
  924.9 59.6 %all-reduce.14 = bf16[256,256]{0,1:T(8,128)(2,1)S(1)} all-reduce(f32[256,256]{0,1:T(8,128)S(1)} %convolution_bitcast_fusion.2), channel_id=1, replica_groups=mesh['prow'=32,'pcol'=16] {'pcol'}, use_global_device_ids=true, to_apply=%region_13.14 | all-reduce | flops 65536 | bytes 393216 | tf_op jit(solution)/shard_map/psum | solution.py:83
  984.5 0.1 constant_dynamic-slice_fusion.2
  984.6 0.1 copy.8
  984.7 0.2 convolution_add_fusion
  984.9 104.2 %psum.126 = f32[16,256]{1,0:T(8,128)S(1)} all-reduce(f32[16,256]{1,0:T(8,128)S(1)} %convolution_add_fusion), channel_id=1, replica_groups=mesh['prow'=32,'pcol'=16] {'prow'}, use_global_device_ids=true, to_apply=%region_14.15 | all-reduce | flops 4096 | bytes 32768 | tf_op jit(solution)/shard_map/psum | solution.py:75
  1089.1 0.3 convolution_bitcast_fusion.1
  1089.5 58.6 %all-reduce.15 = bf16[256,256]{0,1:T(8,128)(2,1)S(1)} all-reduce(f32[256,256]{0,1:T(8,128)S(1)} %convolution_bitcast_fusion.1), channel_id=1, replica_groups=mesh['prow'=32,'pcol'=16] {'pcol'}, use_global_device_ids=true, to_apply=%region_15.16 | all-reduce | flops 65536 | bytes 393216 | tf_op jit(solution)/shard_map/psum | solution.py:83
  1148.0 0.1 dynamic-slice_convert_fusion
  1148.1 0.1 copy.7
  1148.2 0.6 pad_maximum_fusion
  1148.9 1.6 fusion.13
  (11 shorter events, 0.2 us)
Async XLA Ops:
  7.2 136.9 %copy-start = (bf16[256,256]{1,0:T(8,128)(2,1)S(1)}, bf16[256,256]{1,0:T(8,128)(2,1)}, u32[]{:S(2)}) copy-start(bf16[256,256]{1,0:T(8,128)(2,1)} %param.8) | copy-start | bytes 393220
  7.2 195.0 %copy-start.1 = (bf16[4,16,256]{2,1,0:T(8,128)(2,1)S(1)}, bf16[4,16,256]{2,1,0:T(8,128)(2,1)}, u32[]{:S(2)}) copy-start(bf16[4,16,256]{2,1,0:T(8,128)(2,1)} %param.7) | copy-start | bytes 98308
  7.2 498.4 %all-gather.2.cloned.1.call-start = ((), (), s32[]{:S(2)}) async-start(), calls=%async_computation.1 | async-start | bytes 2228224 | tf_op jit(solution)/shard_map/all_gather | solution.py:58
  7.9 1140.9 %reduce-scatter.2.cloned.1.call-start = ((), (), s32[]{:S(2)}) async-start(), calls=%async_computation.2 | async-start | bytes 4456448 | tf_op jit(solution)/shard_map/reduce_scatter | solution.py:50
Sparse Core Ops, SparseCore 0:
  11.0 65.0 all-gather.1
  505.7 85.3 reduce-scatter.1
where the time goes:
time: 1170 us; the launch traced here: 1160 us
  blocking collectives  1130 us (97%)
  between operations  14.3 us (1%)
    psum x4, blocking collectives, on_device(): column_total = lax.psum(term, 'prow')  401 us
    psum x4, blocking collectives, from_root(): return lax.psum(block, axis)  250 us
    psum x4, blocking collectives, on_device(): residual = lax.psum(running, 'pcol')  240 us
    psum x4, blocking collectives, on_device(): combined = lax.psum(applied, 'pcol')  237 us
  transfers between devices with their start and end apart: 2, of which 0 were waited for; matrix products, arithmetic and copies ran while one was open for 1% of the time, Pallas kernels for 0%

commit v1 on v0

v1 whole, which is shorter than its diff:
```python
import jax
import jax.numpy as jnp
from jax import lax
from jax.experimental import pallas as pl
from jax.experimental.pallas import tpu as pltpu
from jax.sharding import PartitionSpec as P

ROOT = 0
F32 = jnp.float32
BF16 = jnp.bfloat16


def dot(a, b, ca=1, cb=0):
    return lax.dot_general(a, b, (((ca,), (cb,)), ((), ())), preferred_element_type=F32)


def remote(src, dst, send_sem, recv_sem, **device):
    return pltpu.make_async_remote_copy(
        src_ref=src,
        dst_ref=dst,
        send_sem=send_sem,
        recv_sem=recv_sem,
        device_id=device,
        device_id_type=pl.DeviceIdType.MESH,
    )


def signal(sem, **device):
    pl.semaphore_signal(sem, inc=1, device_id=device, device_id_type=pl.DeviceIdType.MESH)


def kernel(rows_n, cols_n, panels, width, *refs):
    factor, pattern, diag, right, later, sol_out, red_out = refs[:7]
    (
        full, inv, lead_own, lead, rt_slabs, rt_own, rt_all, bulk, bulk_in, z_own, z_in,
        y_own, y_all, s_own, s_all, out_buf, right_v, later_v,
    ) = refs[7:25]
    (
        loc, bar_unused, fa, fb, da, db, la, lb, ga, gb, ra, rb, qa, qb, sa, sb, za, zb,
        ya, yb, va, vb, ta, tb, oa, ob,
    ) = refs[25:]
    del bar_unused
    row = lax.axis_index("prow")
    col = lax.axis_index("pcol")
    narrow = width // cols_n
    is_root = row == ROOT

    copies = [
        pltpu.make_async_copy(right, right_v, loc.at[0]),
        pltpu.make_async_copy(later, later_v, loc.at[1]),
    ]
    for copy in copies:
        copy.start()

    barrier = pltpu.get_barrier_semaphore()

    def greet_col(i, _):
        signal(barrier, pcol=lax.rem(col + i, cols_n))
        return 0

    def greet_row(i, _):
        signal(barrier, prow=lax.rem(row + i, rows_n))
        return 0

    lax.fori_loop(1, cols_n, greet_col, 0)

    @pl.when(is_root)
    def _():
        lax.fori_loop(1, rows_n, greet_row, 0)
        pl.semaphore_wait(barrier, cols_n - 1 + rows_n - 1)

    @pl.when(row != ROOT)
    def _():
        signal(barrier, prow=ROOT)
        pl.semaphore_wait(barrier, cols_n)

    def strip(ref, j):
        return ref.at[:, pl.ds(pl.multiple_of(j * narrow, narrow), narrow), :]

    def pcol_each(make, what):
        def step(i, _):
            getattr(make(i, lax.rem(col + i, cols_n)), what)()
            return 0

        lax.fori_loop(1, cols_n, step, 0)

    class Exchange:
        def __init__(self, src, dst, send, recv):
            self.src, self.dst, self.send, self.recv = src, dst, send, recv

        def start(self):
            pcol_each(
                lambda i, j: remote(
                    self.src(j), self.dst(col), self.send.at[i], self.recv.at[col], pcol=j
                ),
                "start",
            )

        def arrive(self):
            pcol_each(
                lambda i, j: remote(
                    self.src(j), self.dst(j), self.send.at[i], self.recv.at[j], pcol=j
                ),
                "wait_recv",
            )

        def drain(self):
            pcol_each(
                lambda i, j: remote(
                    self.src(j), self.dst(j), self.send.at[i], self.recv.at[j], pcol=j
                ),
                "wait_send",
            )

    def factor_block(j):
        return factor.at[:, :, pl.ds(pl.multiple_of(j * width, width), width)]

    factor_x = Exchange(factor_block, lambda j: strip(full, j), fa, fb)
    inv_x = Exchange(lambda j: diag, lambda j: strip(inv, j), da, db)
    lead_x = Exchange(lambda j: lead_own, lambda j: strip(lead, j), ga, gb)
    bulk_x = Exchange(lambda j: bulk.at[j], lambda j: bulk_in.at[j], sa, sb)
    y_x = Exchange(lambda j: y_own, lambda j: y_all.at[j], va, vb)
    sol_x = Exchange(lambda j: s_own, lambda j: s_all.at[j], ta, tb)

    def lead_copy(q):
        first = q * (q - 1) // 2
        return remote(
            factor.at[pl.ds(0, q), :, pl.ds(0, width)],
            lead_own.at[pl.ds(first, q)],
            la,
            lb.at[q],
            prow=ROOT,
        )

    for q in range(1, panels):

        @pl.when(row == q)
        def _(q=q):
            lead_copy(q).start()

    factor_x.start()
    own_factor = pltpu.make_async_copy(factor_block(col), strip(full, col), loc.at[2])
    own_factor.start()

    @pl.when(is_root)
    def _():
        inv_x.start()
        pltpu.make_async_copy(diag, strip(inv, col), loc.at[3]).start()

    for copy in copies:
        copy.wait()

    def rt_scatter(j):
        return remote(rt_slabs.at[j], rt_own, ra.at[j], rb, pcol=j)

    @pl.when((row < panels) & (col == 0))
    def _():
        flipped = right_v[...].astype(F32).T.astype(BF16)
        rt_slabs[...] = flipped.reshape(rt_slabs.shape)

        def step(j, _):
            rt_scatter(j).start()
            return 0

        lax.fori_loop(1, cols_n, step, 0)
        rt_own[...] = rt_slabs[0]

    @pl.when((row < panels) & (col != 0))
    def _():
        rt_scatter(0).wait_recv()

    for q in range(1, panels):

        @pl.when(row == q)
        def _(q=q):
            remote(rt_own, rt_all.at[q], qa, qb.at[q], prow=ROOT).start()

    later_t = later_v[...].astype(F32).T.astype(BF16)

    @pl.when(is_root)
    def _():
        rt_all[0] = rt_own[...]
        for q in range(1, panels):
            lead_copy(q).wait_recv()
        lead_x.start()
        pltpu.make_async_copy(lead_own, strip(lead, col), loc.at[4]).start()

    factor_x.arrive()
    own_factor.wait()
    scales = [pattern[col, p].astype(F32) for p in range(panels)]
    outside = jnp.where((row < panels) & (col == 0), 0.0, 1.0).astype(F32)
    for p in range(panels):
        part = dot(later_t, full[p], 1, 1) * (scales[p] * outside)
        bulk[:, :, p * width : (p + 1) * width] = part.astype(BF16).reshape(
            cols_n, narrow, width
        )
    bulk_x.start()

    def y_send(r):
        return remote(y_own, y_own, ya.at[r], yb, prow=r)

    @pl.when(is_root)
    def _():
        inv_x.arrive()
        pltpu.make_async_copy(diag, strip(inv, col), loc.at[3]).wait()
        lead_x.arrive()
        pltpu.make_async_copy(lead_own, strip(lead, col), loc.at[4]).wait()
        solved = []
        for q in range(panels):
            if q > 0:
                remote(rt_own, rt_all.at[q], qa, qb.at[q], prow=ROOT).wait_recv()
            residual = rt_all[q].astype(F32)
            for p in range(q):
                residual = residual - dot(solved[p], lead[q * (q - 1) // 2 + p])
            y_p = dot(residual.astype(BF16), inv[q], 1, 1).astype(BF16)
            solved.append(y_p)
            y_own[:, q * width : (q + 1) * width] = y_p

        def step(r, _):
            y_send(r).start()
            return 0

        lax.fori_loop(1, rows_n, step, 0)
        y_x.start()

    bulk_x.arrive()
    total = bulk[col].astype(F32)
    for i in range(1, cols_n):
        total = total + bulk_in[lax.rem(col + i, cols_n)].astype(F32)

    def z_send(r):
        return remote(z_own, z_in.at[r], za, zb.at[r], prow=ROOT)

    @pl.when(row != ROOT)
    def _():
        z_own[...] = total.astype(BF16)
        z_send(row).start()
        y_send(0).wait_recv()
        y_x.start()

    def out_send(r):
        return remote(out_buf, out_buf, oa.at[r], ob, prow=r)

    @pl.when(is_root)
    def _():
        gathered = total
        for r in range(1, rows_n):
            z_send(r).wait_recv()
            gathered = gathered + z_in[r].astype(F32)
        answers = [None] * panels
        for p in reversed(range(panels)):
            column = gathered[:, p * width : (p + 1) * width]
            for q in range(panels - 1, p, -1):
                column = column + dot(answers[q], lead[q * (q - 1) // 2 + p], 1, 1)
            gap = y_own[:, p * width : (p + 1) * width].astype(F32) - column
            high = gap.astype(BF16)
            rest = gap - high.astype(F32)
            middle = rest.astype(BF16)
            low = (rest - middle.astype(F32)).astype(BF16)
            applied = dot(high, inv[p]) + (dot(middle, inv[p]) + dot(low, inv[p]))
            answers[p] = applied.astype(BF16)
            s_own[:, p * width : (p + 1) * width] = answers[p]
        sol_x.start()
        s_all[col] = s_own[...]
        sol_x.arrive()
        mine = lax.broadcasted_iota(jnp.int32, (narrow, width), 0) + col * narrow
        pick = (lax.broadcasted_iota(jnp.int32, (narrow, width), 1) == mine).astype(BF16)
        for p in range(panels):
            block = s_all[:, :, p * width : (p + 1) * width].reshape(-1, width)
            out_buf[p] = dot(pick, block, 1, 1).astype(BF16)

        def step(r, _):
            out_send(r).start()
            return 0

        lax.fori_loop(1, rows_n, step, 0)
        sol_out[...] = out_buf[...]

    y_all[col] = y_own[...]
    y_x.arrive()
    lower_t = jnp.zeros((width, width), F32)
    for p in range(panels):
        y_p = y_all[:, :, p * width : (p + 1) * width].reshape(-1, width)
        lower_t = lower_t + dot(y_p, full[p]) * scales[p]
    red_out[...] = (right_v[...].astype(F32) - lower_t.T).astype(BF16)

    @pl.when(row != ROOT)
    def _():
        out_send(0).wait_recv()
        sol_out[...] = out_buf[...]

    factor_x.drain()
    bulk_x.drain()
    y_x.drain()

    @pl.when((row < panels) & (col == 0))
    def _():
        def step(j, _):
            rt_scatter(j).wait_send()
            return 0

        lax.fori_loop(1, cols_n, step, 0)

    for q in range(1, panels):

        @pl.when(row == q)
        def _(q=q):
            lead_copy(q).wait_send()
            remote(rt_own, rt_all.at[q], qa, qb.at[q], prow=ROOT).wait_send()

    @pl.when(row != ROOT)
    def _():
        z_send(row).wait_send()

    @pl.when(is_root)
    def _():
        inv_x.drain()
        lead_x.drain()
        sol_x.drain()

        def step(r, _):
            y_send(r).wait_send()
            out_send(r).wait_send()
            return 0

        lax.fori_loop(1, rows_n, step, 0)


def solution(mesh):
    rows_n, cols_n = mesh.shape["prow"], mesh.shape["pcol"]

    def on_device(factor_t, pattern, diag_inverse, right_side, later_solution):
        panels, narrow, _ = factor_t.shape
        width = diag_inverse.shape[2]
        rhs = right_side.shape[1]
        pairs = panels * (panels - 1) // 2
        slab = (rhs // cols_n, panels * width)
        dma = pltpu.SemaphoreType.DMA
        per_col, per_row = dma((cols_n,)), dma((rows_n,))
        vmem = pltpu.VMEM
        scratch = [
            vmem((panels, width, width), BF16),
            vmem((panels, width, width), BF16),
            vmem((pairs, narrow, width), BF16),
            vmem((pairs, width, width), BF16),
            vmem((cols_n, rhs // cols_n, width), BF16),
            vmem((rhs // cols_n, width), BF16),
            vmem((panels, rhs // cols_n, width), BF16),
            vmem((cols_n,) + slab, BF16),
            vmem((cols_n,) + slab, BF16),
            vmem(slab, BF16),
            vmem((rows_n,) + slab, BF16),
            vmem(slab, BF16),
            vmem((cols_n,) + slab, BF16),
            vmem(slab, BF16),
            vmem((cols_n,) + slab, BF16),
            vmem((panels, narrow, rhs), BF16),
            vmem(right_side.shape, BF16),
            vmem(later_solution.shape, BF16),
            dma((8,)),
            dma,
            per_col, per_col,
            per_col, per_col,
            dma, dma((panels,)),
            per_col, per_col,
            per_col, dma,
            dma, dma((panels,)),
            per_col, per_col,
            dma, per_row,
            per_row, dma,
            per_col, per_col,
            per_col, per_col,
            per_row, dma,
        ]
        anywhere = pl.BlockSpec(memory_space=pl.ANY)
        return pl.pallas_call(
            lambda *refs: kernel(rows_n, cols_n, panels, width, *refs),
            out_shape=(
                jax.ShapeDtypeStruct((panels, narrow, rhs), BF16),
                jax.ShapeDtypeStruct(right_side.shape, BF16),
            ),
            in_specs=[
                anywhere,
                pl.BlockSpec(memory_space=pltpu.SMEM),
                anywhere,
                anywhere,
                anywhere,
            ],
            out_specs=(
                pl.BlockSpec(memory_space=pltpu.VMEM),
                pl.BlockSpec(memory_space=pltpu.VMEM),
            ),
            scratch_shapes=scratch,
            compiler_params=pltpu.CompilerParams(
                collective_id=0, has_side_effects=True, vmem_limit_bytes=48 << 20
            ),
            name="solve",
        )(factor_t, pattern, diag_inverse, right_side, later_solution)

    in_specs = (
        P(None, "pcol", "prow"),
        P("prow", None),
        P(None, "pcol", None),
        P(("prow", "pcol"), None),
        P(("prow", "pcol"), None),
    )
    out_specs = (P(None, "pcol", None), P(("prow", "pcol"), None))
    return jax.shard_map(
        on_device, mesh=mesh, in_specs=in_specs, out_specs=out_specs, check_vma=False
    )
```

time: 1170 us -> 65.1 us (0.06)
  the two profiles are of different devices: /device:TPU:1 before, /device:TPU:24 now
where the time goes in v1:
time: 65.1 us; the launch traced here: 64.8 us
  Pallas kernels  58.5 us (90%)
  local copies, waits for them, and re-layouts  5.64 us (9%)
    pallas_call x1, Pallas kernels, on_device(): pl.pallas_call(lambda *refs: kernel(rows_n, cols_n, panels, width, *refs)...  58.5 us
    unnamed x11, local copies, waits for them, and re-layouts  5.64 us

profile of v1, /device:TPU:24, one launch (start us, length us, event | category | flops | bytes accessed | tf_op | source)
XLA Modules:
  0.0 64.8 jit_solution(1843347827512452063)
XLA Ops:
  0.6 0.8 %copy.7.refs_1_ = s32[16,4]{1,0:T(8,128)S(1)} copy(s32[16,4]{0,1:T(4,128)} %param.6) | data formatting | bytes 512 | tf_op args[1]
  1.4 0.0 copy-start
  1.4 1.0 %copy-done = bf16[4,16,4096]{2,1,0:T(8,128)(2,1)S(1)} copy-done((bf16[4,16,4096]{2,1,0:T(8,128)(2,1)S(1)}, bf16[4,16,4096]{2,1,0:T(8,128)(2,1)}, u32[]{:S(2)}) %copy-start) | copy-done | bytes 524312
  2.4 0.0 copy-start.1
  2.4 0.9 %copy-done.1 = bf16[256,256]{1,0:T(8,128)(2,1)S(1)} copy-done((bf16[256,256]{1,0:T(8,128)(2,1)S(1)}, bf16[256,256]{1,0:T(8,128)(2,1)}, u32[]{:S(2)}) %copy-start.1) | copy-done | bytes 131096
  3.3 0.0 copy-start.2
  3.3 0.9 %copy-done.2 = bf16[256,256]{1,0:T(8,128)(2,1)S(1)} copy-done((bf16[256,256]{1,0:T(8,128)(2,1)S(1)}, bf16[256,256]{1,0:T(8,128)(2,1)}, u32[]{:S(2)}) %copy-start.2) | copy-done | bytes 131096
  4.2 0.0 copy-start.3
  4.2 0.8 %copy-done.3 = bf16[4,16,256]{2,1,0:T(8,128)(2,1)S(1)} copy-done((bf16[4,16,256]{2,1,0:T(8,128)(2,1)S(1)}, bf16[4,16,256]{2,1,0:T(8,128)(2,1)}, u32[]{:S(2)}) %copy-start.3) | copy-done | bytes 32792
  5.0 58.5 %solve.1 = (bf16[4,16,256]{2,1,0:T(8,128)(2,1)S(1)}, bf16[256,256]{1,0:T(8,128)(2,1)S(1)}) custom-call(bf16[4,16,4096]{2,1,0:T(8,128)(2,1)S(1)} %copy-done, s32[16,4]{1,0:T(8,128)S(1)} %copy.7.refs_1_, bf16[4,16,256]{2,1,0:T(8,128)(2,1)S(1)} %copy-done.3, bf16[256,256]{1,0:T(8,128)(2,1)S(1)} %copy-done.1, bf16[256,256]{1,0:T(8,128)(2,1)S(1)} %copy-done.2), custom_call_target="tpu_custom_call" | custom-call | tf_op jit(solution)/shard_map/solve/pallas_call | solution.py:376
  63.5 0.6 copy.10
  64.1 0.7 %copy.11 = bf16[256,256]{1,0:T(8,128)(2,1)} copy(bf16[256,256]{1,0:T(8,128)(2,1)S(1)} %get-tuple-element.5) | data formatting | bytes 262144
Async XLA Ops:
  1.4 1.0 %copy-start = (bf16[4,16,4096]{2,1,0:T(8,128)(2,1)S(1)}, bf16[4,16,4096]{2,1,0:T(8,128)(2,1)}, u32[]{:S(2)}) copy-start(bf16[4,16,4096]{2,1,0:T(8,128)(2,1)} %refs_0_.1) | copy-start | bytes 1572868
  2.4 0.9 %copy-start.1 = (bf16[256,256]{1,0:T(8,128)(2,1)S(1)}, bf16[256,256]{1,0:T(8,128)(2,1)}, u32[]{:S(2)}) copy-start(bf16[256,256]{1,0:T(8,128)(2,1)} %refs_3_.1) | copy-start | bytes 393220
  3.3 0.9 %copy-start.2 = (bf16[256,256]{1,0:T(8,128)(2,1)S(1)}, bf16[256,256]{1,0:T(8,128)(2,1)}, u32[]{:S(2)}) copy-start(bf16[256,256]{1,0:T(8,128)(2,1)} %refs_4_.1) | copy-start | bytes 393220
  4.2 0.8 %copy-start.3 = (bf16[4,16,256]{2,1,0:T(8,128)(2,1)S(1)}, bf16[4,16,256]{2,1,0:T(8,128)(2,1)}, u32[]{:S(2)}) copy-start(bf16[4,16,256]{2,1,0:T(8,128)(2,1)} %refs_2_.1) | copy-start | bytes 98308

commit v2 on v1

v2 whole, which is shorter than its diff:
```python
import math

import jax
import jax.numpy as jnp
from jax import lax
from jax.experimental import pallas as pl
from jax.experimental.pallas import tpu as pltpu
from jax.sharding import PartitionSpec as P

ROOT = 0
F32 = jnp.float32
BF16 = jnp.bfloat16


def dot(a, b, ca=1, cb=0):
    return lax.dot_general(a, b, (((ca,), (cb,)), ((), ())), preferred_element_type=F32)


def remote(src, dst, send_sem, recv_sem, **device):
    return pltpu.make_async_remote_copy(
        src_ref=src,
        dst_ref=dst,
        send_sem=send_sem,
        recv_sem=recv_sem,
        device_id=device,
        device_id_type=pl.DeviceIdType.MESH,
    )


def signal(sem, **device):
    pl.semaphore_signal(sem, inc=1, device_id=device, device_id_type=pl.DeviceIdType.MESH)


def kernel(rows_n, cols_n, panels, width, *refs):
    factor, pattern, diag, right, later, sol_out, red_out = refs[:7]
    (
        part, later_all, inv, lead_own, lead, rt_slabs, rt_own, rt_all, bulk, bulk_in, z_own,
        z_in, y_own, y_keep, y_all, low, low_in, spread, sol_in, out_buf, right_v, acc,
    ) = refs[7:29]
    (
        loc, hello, fa, fb, ha, hb, da, db, la, lb, ga, gb, ra, rb, qa, qb, sa, sb, za, zb,
        ya, yb, va, vb, wa, wb, ta, tb, oa, ob,
    ) = refs[29:]
    row = lax.axis_index("prow")
    col = lax.axis_index("pcol")
    side = math.isqrt(cols_n)
    x, y = lax.div(col, side), lax.rem(col, side)
    narrow = width // cols_n
    group = side * narrow
    quarter = side * width
    is_root = row == ROOT

    fetch = pltpu.make_async_copy(right, right_v, loc.at[0])
    fetch.start()

    barrier = pltpu.get_barrier_semaphore()

    def greet_col(i, _):
        signal(barrier, pcol=lax.rem(col + i, cols_n))
        return 0

    def greet_row(i, _):
        signal(barrier, prow=lax.rem(row + i, rows_n))
        return 0

    lax.fori_loop(1, cols_n, greet_col, 0)
    @pl.when(is_root)
    def _():
        lax.fori_loop(1, rows_n, greet_row, 0)

    @pl.when(lax.rem(row, 2) == 1)
    def _():
        signal(barrier, prow=row - 1)

    expected = cols_n - 1 + jnp.where(is_root, 0, 1) + (1 - lax.rem(row, 2))
    pl.semaphore_wait(barrier, expected)

    def strip(ref, j):
        return ref.at[:, pl.ds(pl.multiple_of(j * narrow, narrow), narrow), :]

    class Exchange:
        def __init__(self, count, peer, src, dst, send, recv, me):
            self.count, self.peer, self.src, self.dst = count, peer, src, dst
            self.send, self.recv, self.me = send, recv, me

        def each(self, what):
            def step(i, _):
                device, j = self.peer(i)
                to = self.me if what == "start" else j
                getattr(
                    remote(
                        self.src(j), self.dst(to), self.send.at[i], self.recv.at[to], pcol=device
                    ),
                    what,
                )()
                return 0

            lax.fori_loop(1, self.count, step, 0)

        def start(self):
            self.each("start")

        def arrive(self):
            self.each("wait_recv")

        def drain(self):
            self.each("wait_send")

    def any_peer(i):
        j = lax.rem(col + i, cols_n)
        return j, j

    def x_peer(i):
        j = lax.rem(x + i, side)
        return j * side + y, j

    def y_peer(i):
        j = lax.rem(y + i, side)
        return x * side + j, j

    def over_all(src, dst, send, recv):
        return Exchange(cols_n, any_peer, src, dst, send, recv, col)

    def turned(j):
        return lax.rem(j, side) * side + lax.div(j, side)

    def factor_quarter(j):
        return factor.at[:, :, pl.ds(pl.multiple_of(j * quarter, quarter), quarter)]

    def later_strip(j):
        return later_all.at[pl.ds(pl.multiple_of(j * width, width), width), :]

    factor_x = Exchange(
        side, x_peer, factor_quarter, lambda j: strip(part, j), fa, fb, x
    )
    later_x = Exchange(side, y_peer, lambda j: later, later_strip, ha, hb, y)
    inv_x = over_all(lambda j: diag, lambda j: strip(inv, turned(j)), da, db)
    lead_x = over_all(lambda j: lead_own, lambda j: strip(lead, turned(j)), ga, gb)
    bulk_x = over_all(lambda j: bulk.at[j], lambda j: bulk_in.at[j], sa, sb)
    y_x = over_all(lambda j: y_own.at[lax.rem(j, side)], lambda j: y_all.at[j], va, vb)
    low_x = Exchange(
        side, y_peer, lambda j: low.at[j], lambda j: low_in.at[j], wa, wb, y
    )
    sol_x = over_all(lambda j: strip(spread, j), lambda j: sol_in.at[j], ta, tb)

    factor_x.start()
    later_x.start()
    own_copies = [
        pltpu.make_async_copy(factor_quarter(x), strip(part, x), loc.at[1]),
        pltpu.make_async_copy(later, later_strip(y), loc.at[2]),
    ]
    for copy in own_copies:
        copy.start()

    @pl.when(row != ROOT)
    def _():
        signal(hello, prow=ROOT)

    def lead_copy(q):
        first = q * (q - 1) // 2
        return remote(
            factor.at[pl.ds(0, q), :, pl.ds(0, width)],
            lead_own.at[pl.ds(first, q)],
            la,
            lb.at[q],
            prow=ROOT,
        )

    for q in range(1, panels):

        @pl.when(row == q)
        def _(q=q):
            lead_copy(q).start()

    @pl.when(is_root)
    def _():
        inv_x.start()
        pltpu.make_async_copy(diag, strip(inv, turned(col)), loc.at[3]).start()

    fetch.wait()

    def rt_scatter(j):
        return remote(rt_slabs.at[j], rt_own, ra.at[j], rb, pcol=j)

    @pl.when((row < panels) & (col == 0))
    def _():
        flipped = right_v[...].astype(F32).T.astype(BF16)
        rt_slabs[...] = flipped.reshape(rt_slabs.shape)

        def step(j, _):
            rt_scatter(j).start()
            return 0

        lax.fori_loop(1, cols_n, step, 0)
        rt_own[...] = rt_slabs[0]

    @pl.when((row < panels) & (col != 0))
    def _():
        rt_scatter(0).wait_recv()

    def rt_send(q):
        return remote(rt_own, rt_all.at[q], qa, qb.at[q], prow=ROOT)

    for q in range(1, panels):

        @pl.when(row == q)
        def _(q=q):
            rt_send(q).start()

    @pl.when(is_root)
    def _():
        rt_all[0] = rt_own[...]
        for q in range(1, panels):
            lead_copy(q).wait_recv()
        lead_x.start()
        pltpu.make_async_copy(lead_own, strip(lead, turned(col)), loc.at[4]).start()

    factor_x.arrive()
    later_x.arrive()
    for copy in own_copies:
        copy.wait()
    columns = panels * group

    @pl.when((row < panels) & (x == 0))
    def _():
        later_all[:width, :] = jnp.zeros((width, later_all.shape[1]), BF16)

    acc[...] = jnp.zeros_like(acc)

    def block_of(b):
        return pl.ds(pl.multiple_of(b * width, width), width)

    def bulk_step(b, _):
        rows = block_of(b)
        pieces = []
        for p in range(panels):
            keep = pattern[p, x * side + b].astype(F32).astype(BF16)
            piece = part[p, :, rows] * keep
            part[p, :, rows] = piece
            pieces.append(piece)
        acc[...] += dot(jnp.concatenate(pieces, axis=0), later_all[rows, :])
        return 0

    lax.fori_loop(0, side, bulk_step, 0)
    bulk[...] = acc[...].T.astype(BF16).reshape(bulk.shape)
    bulk_x.start()
    bulk_in[col] = bulk[col]

    chips = rows_n // 2

    def along_row(send):
        def step(i, _):
            send(2 * i).start()
            return 0

        lax.fori_loop(1, chips, step, 0)
        send(1).start()

    first_core = lax.rem(row, 2) == 0
    relays = first_core & (row != ROOT)

    def y_send(r):
        return remote(y_own, y_own, ya.at[r], yb, prow=r)

    @pl.when(is_root)
    def _():
        inv_x.arrive()
        pltpu.make_async_copy(diag, strip(inv, turned(col)), loc.at[3]).wait()
        lead_x.arrive()
        pltpu.make_async_copy(lead_own, strip(lead, turned(col)), loc.at[4]).wait()
        solved = []
        for q in range(panels):
            if q > 0:
                rt_send(q).wait_recv()
            residual = rt_all[q].astype(F32)
            for p in range(q):
                residual = residual - dot(solved[p], lead[q * (q - 1) // 2 + p])
            y_q = dot(residual.astype(BF16), inv[q], 1, 1).astype(BF16)
            solved.append(y_q)
            y_keep[q] = y_q
        for j in range(side):
            pieces = [y_q[:, j * group : (j + 1) * group] for y_q in solved]
            y_own[j] = jnp.concatenate(pieces, axis=1)
        pl.semaphore_wait(hello, rows_n - 1)

        along_row(y_send)
        y_x.start()

    bulk_x.arrive()
    def sum_step(i, sums):
        return tuple(t + bulk_in[i * side + j].astype(F32) for j, t in enumerate(sums))

    sums = lax.fori_loop(
        1, side, sum_step, tuple(bulk_in[j].astype(F32) for j in range(side))
    )
    for p in range(panels):
        pieces = [total[:, p * group : (p + 1) * group] for total in sums]
        z_own[p] = jnp.concatenate(pieces, axis=1).astype(z_own.dtype)

    def z_send(r):
        return remote(z_own, z_in.at[r], za, zb.at[r], prow=ROOT)

    @pl.when(row != ROOT)
    def _():
        z_send(row).start()
        y_send(0).wait_recv()

        @pl.when(relays)
        def _():
            y_send(row + 1).start()

        y_x.start()

    def out_send(r):
        return remote(out_buf, out_buf, oa.at[r], ob, prow=r)

    @pl.when(is_root)
    def _():
        def gather_step(r, sums):
            z_send(r).wait_recv()
            return tuple(t + z_in[r, p].astype(F32) for p, t in enumerate(sums))

        gathered = lax.fori_loop(
            1, rows_n, gather_step, tuple(z_own[p].astype(F32) for p in range(panels))
        )
        answers = [None] * panels
        shift = lax.rem(col, cols_n // 2) * narrow
        shape = (narrow, 128)
        at = lax.broadcasted_iota(jnp.int32, shape, 0) + shift
        place = (lax.broadcasted_iota(jnp.int32, shape, 1) == at).astype(BF16)
        for p in reversed(range(panels)):
            column = gathered[p]
            for q in range(panels - 1, p, -1):
                column = column + dot(answers[q], lead[q * (q - 1) // 2 + p], 1, 1)
            gap = y_keep[p].astype(F32) - column
            high = gap.astype(BF16)
            rest = gap - high.astype(F32)
            middle = rest.astype(BF16)
            lowest = (rest - middle.astype(F32)).astype(BF16)
            parts = dot(jnp.concatenate([high, middle, lowest], axis=0), inv[p])
            applied = parts[:narrow] + (parts[narrow : 2 * narrow] + parts[2 * narrow :])
            answers[p] = applied.astype(BF16)
            spread[p] = dot(answers[p], place, 0, 0).astype(BF16)
        sol_x.start()
        mine = pl.ds(pl.multiple_of(col * narrow, narrow), narrow)
        sol_in[col] = spread[:, mine, :]

    y_all[col] = y_own[y]
    y_x.arrive()

    def lower_step(j, _):
        strip_j = part[:, :, block_of(j)].reshape(columns, width)
        low[j] = dot(y_all[...].reshape(-1, columns), strip_j).astype(BF16)
        return 0

    lax.fori_loop(0, side, lower_step, 0)
    low_x.start()
    low_in[y] = low[y]

    @pl.when(is_root)
    def _():
        sol_x.arrive()
        half = cols_n // 2

        def merge_step(j, sums):
            first, second = sums
            return first + sol_in[j].astype(F32), second + sol_in[half + j].astype(F32)

        merged = lax.fori_loop(
            1, half, merge_step, (sol_in[0].astype(F32), sol_in[half].astype(F32))
        )
        out_buf[:, :, :128] = merged[0].astype(BF16)
        out_buf[:, :, 128:] = merged[1].astype(BF16)

        along_row(out_send)

    low_x.arrive()
    lower_t = low_in[0].astype(F32)
    for j in range(1, side):
        lower_t = lower_t + low_in[j].astype(F32)
    red_out[...] = (right_v[...].astype(F32) - lower_t.T).astype(BF16)

    @pl.when(row != ROOT)
    def _():
        out_send(0).wait_recv()

        @pl.when(relays)
        def _():
            out_send(row + 1).start()

    sol_out[...] = out_buf[...]

    for exchange in (factor_x, later_x, bulk_x, y_x, low_x):
        exchange.drain()

    @pl.when((row < panels) & (col == 0))
    def _():
        def step(j, _):
            rt_scatter(j).wait_send()
            return 0

        lax.fori_loop(1, cols_n, step, 0)

    for q in range(1, panels):

        @pl.when(row == q)
        def _(q=q):
            lead_copy(q).wait_send()
            rt_send(q).wait_send()

    @pl.when(row != ROOT)
    def _():
        z_send(row).wait_send()

    @pl.when(is_root)
    def _():
        inv_x.drain()
        lead_x.drain()
        sol_x.drain()

        def step(i, _):
            y_send(2 * i).wait_send()
            out_send(2 * i).wait_send()
            return 0

        lax.fori_loop(1, chips, step, 0)

    @pl.when(first_core)
    def _():
        y_send(row + 1).wait_send()
        out_send(row + 1).wait_send()


def solution(mesh):
    rows_n, cols_n = mesh.shape["prow"], mesh.shape["pcol"]

    def on_device(factor_t, pattern, diag_inverse, right_side, later_solution):
        panels, narrow, _ = factor_t.shape
        width = diag_inverse.shape[2]
        rhs = right_side.shape[1]
        pairs = panels * (panels - 1) // 2
        side = math.isqrt(cols_n)
        group, quarter = side * narrow, side * width
        own = rhs // cols_n
        dma = pltpu.SemaphoreType.DMA
        per_col, per_row, per_side = dma((cols_n,)), dma((rows_n,)), dma((side,))
        vmem = pltpu.VMEM
        scratch = [
            vmem((panels, group, quarter), BF16),
            vmem((quarter, rhs), BF16),
            vmem((panels, width, width), BF16),
            vmem((pairs, narrow, width), BF16),
            vmem((pairs, width, width), BF16),
            vmem((cols_n, own, width), BF16),
            vmem((own, width), BF16),
            vmem((panels, own, width), BF16),
            vmem((cols_n, own, panels * group), BF16),
            vmem((cols_n, own, panels * group), BF16),
            vmem((panels, own, width), BF16),
            vmem((rows_n, panels, own, width), BF16),
            vmem((side, own, panels * group), BF16),
            vmem((panels, own, width), BF16),
            vmem((cols_n, own, panels * group), BF16),
            vmem((side, rhs, width), BF16),
            vmem((side, rhs, width), BF16),
            vmem((panels, width, 128), BF16),
            vmem((cols_n, panels, narrow, 128), BF16),
            vmem((panels, narrow, rhs), BF16),
            vmem(right_side.shape, BF16),
            vmem((panels * group, rhs), F32),
            dma((8,)),
            pltpu.SemaphoreType.REGULAR,
            per_side, per_side,
            per_side, per_side,
            per_col, per_col,
            dma, dma((panels,)),
            per_col, per_col,
            per_col, dma,
            dma, dma((panels,)),
            per_col, per_col,
            dma, per_row,
            per_row, dma,
            per_col, per_col,
            per_side, per_side,
            per_col, per_col,
            per_row, dma,
        ]
        anywhere = pl.BlockSpec(memory_space=pl.ANY)
        return pl.pallas_call(
            lambda *refs: kernel(rows_n, cols_n, panels, width, *refs),
            out_shape=(
                jax.ShapeDtypeStruct((panels, narrow, rhs), BF16),
                jax.ShapeDtypeStruct(right_side.shape, BF16),
            ),
            in_specs=[
                anywhere,
                pl.BlockSpec(memory_space=pltpu.SMEM),
                anywhere,
                anywhere,
                anywhere,
            ],
            out_specs=(
                pl.BlockSpec(memory_space=pltpu.VMEM),
                pl.BlockSpec(memory_space=pltpu.VMEM),
            ),
            scratch_shapes=scratch,
            compiler_params=pltpu.CompilerParams(
                collective_id=0, has_side_effects=True, vmem_limit_bytes=62 << 20
            ),
            name="solve",
        )(factor_t, pattern.T, diag_inverse, right_side, later_solution)

    in_specs = (
        P(None, "pcol", "prow"),
        P("prow", None),
        P(None, "pcol", None),
        P(("prow", "pcol"), None),
        P(("prow", "pcol"), None),
    )
    out_specs = (P(None, "pcol", None), P(("prow", "pcol"), None))
    return jax.shard_map(
        on_device, mesh=mesh, in_specs=in_specs, out_specs=out_specs, check_vma=False
    )
```

time: 65.1 us -> 57.1 us (0.88)
  the two profiles are of different devices: /device:TPU:24 before, /device:TPU:33 now
where the time goes in v2:
time: 57.1 us; the launch traced here: 56.9 us
  Pallas kernels  53.3 us (93%)
  local copies, waits for them, and re-layouts  2.94 us (5%)
  between operations  0.64 us (1%)
    pallas_call x1, Pallas kernels, on_device(): pl.pallas_call(lambda *refs: kernel(rows_n, cols_n, panels, width, *refs)...  53.3 us
    unnamed x2, local copies, waits for them, and re-layouts  2.94 us

profile of v2, /device:TPU:33, one launch (start us, length us, event | category | flops | bytes accessed | tf_op | source)
XLA Modules:
  0.0 56.9 jit_solution(377104878723744434)
XLA Ops:
  0.6 53.3 %solve.1 = (bf16[4,16,256]{2,1,0:T(8,128)(2,1)}, bf16[256,256]{1,0:T(8,128)(2,1)}) custom-call(bf16[4,16,4096]{2,1,0:T(8,128)(2,1)} %refs_0_.1, s32[4,16]{1,0:T(4,128)} %bitcast.1, bf16[4,16,256]{2,1,0:T(8,128)(2,1)} %refs_2_.1, bf16[256,256]{1,0:T(8,128)(2,1)} %refs_3_.1, bf16[256,256]{1,0:T(8,128)(2,1)} %refs_4_.1), custom_call_target="tpu_custom_call" | custom-call | tf_op jit(solution)/shard_map/solve/pallas_call | solution.py:489
  53.9 1.4 %copy.9 = bf16[4,16,256]{2,1,0:T(8,128)(2,1)} copy(bf16[4,16,256]{2,1,0:T(8,128)(2,1)} %get-tuple-element.4) | data formatting | bytes 65536
  55.3 1.6 %copy.10 = bf16[256,256]{1,0:T(8,128)(2,1)} copy(bf16[256,256]{1,0:T(8,128)(2,1)} %get-tuple-element.5) | data formatting | bytes 262144

commit v3 on v2

--- a/solution.py
+++ b/solution.py
@@ -32,15 +32,15 @@
 
 
 def kernel(rows_n, cols_n, panels, width, *refs):
-    factor, pattern, diag, right, later, sol_out, red_out = refs[:7]
+    factor, pattern_in, diag, right, later, sol_out, red_out = refs[:7]
     (
         part, later_all, inv, lead_own, lead, rt_slabs, rt_own, rt_all, bulk, bulk_in, z_own,
-        z_in, y_own, y_keep, y_all, low, low_in, spread, sol_in, out_buf, right_v, acc,
-    ) = refs[7:29]
+        z_in, y_own, y_keep, y_all, low, low_in, spread, sol_in, out_buf, right_v, acc, pattern,
+    ) = refs[7:30]
     (
         loc, hello, fa, fb, ha, hb, da, db, la, lb, ga, gb, ra, rb, qa, qb, sa, sb, za, zb,
         ya, yb, va, vb, wa, wb, ta, tb, oa, ob,
-    ) = refs[29:]
+    ) = refs[30:]
     row = lax.axis_index("prow")
     col = lax.axis_index("pcol")
     side = math.isqrt(cols_n)
@@ -52,6 +52,8 @@
 
     fetch = pltpu.make_async_copy(right, right_v, loc.at[0])
     fetch.start()
+    fetch_pattern = pltpu.make_async_copy(pattern_in, pattern, loc.at[5])
+    fetch_pattern.start()
 
     barrier = pltpu.get_barrier_semaphore()
 
@@ -178,6 +180,7 @@
         pltpu.make_async_copy(diag, strip(inv, turned(col)), loc.at[3]).start()
 
     fetch.wait()
+    fetch_pattern.wait()
 
     def rt_scatter(j):
         return remote(rt_slabs.at[j], rt_own, ra.at[j], rb, pcol=j)
@@ -468,6 +471,7 @@
             vmem((panels, narrow, rhs), BF16),
             vmem(right_side.shape, BF16),
             vmem((panels * group, rhs), F32),
+            pltpu.SMEM((panels, pattern.shape[0]), jnp.int32),
             dma((8,)),
             pltpu.SemaphoreType.REGULAR,
             per_side, per_side,
@@ -485,30 +489,28 @@
             per_col, per_col,
             per_row, dma,
         ]
-        anywhere = pl.BlockSpec(memory_space=pl.ANY)
+
+        def stay(operand):
+            return pltpu.with_memory_space_constraint(operand, pltpu.MemorySpace.HBM)
+
+        anywhere = pl.BlockSpec(memory_space=pltpu.MemorySpace.HBM)
         return pl.pallas_call(
             lambda *refs: kernel(rows_n, cols_n, panels, width, *refs),
             out_shape=(
                 jax.ShapeDtypeStruct((panels, narrow, rhs), BF16),
                 jax.ShapeDtypeStruct(right_side.shape, BF16),
             ),
-            in_specs=[
-                anywhere,
-                pl.BlockSpec(memory_space=pltpu.SMEM),
-                anywhere,
-                anywhere,
-                anywhere,
-            ],
+            in_specs=[anywhere] * 5,
             out_specs=(
                 pl.BlockSpec(memory_space=pltpu.VMEM),
                 pl.BlockSpec(memory_space=pltpu.VMEM),
             ),
             scratch_shapes=scratch,
             compiler_params=pltpu.CompilerParams(
-                collective_id=0, has_side_effects=True, vmem_limit_bytes=62 << 20
+                collective_id=0, has_side_effects=True, vmem_limit_bytes=48 << 20
             ),
             name="solve",
-        )(factor_t, pattern.T, diag_inverse, right_side, later_solution)
+        )(stay(factor_t), stay(pattern.T), stay(diag_inverse), stay(right_side), stay(later_solution))
 
     in_specs = (
         P(None, "pcol", "prow"),

time: 57.1 us -> 54 us (0.946)
  local copies, waits for them, and re-layouts: 2.94 us -> 1.27 us
  Pallas kernels: 53.3 us -> 51.9 us
    unnamed x2, local copies, waits for them, and re-layouts: 2.94 us -> 1.27 us
    pallas_call x1, Pallas kernels: 53.3 us -> 51.9 us  [on_device(): pl.pallas_call(lambda *refs: kernel(rows_n, cols_n, panels, width, *refs)...]
where the time goes in v3:
time: 54 us; the launch traced here: 53.8 us
  Pallas kernels  51.9 us (96%)
  local copies, waits for them, and re-layouts  1.27 us (2%)
  between operations  0.64 us (1%)
    pallas_call x1, Pallas kernels, on_device(): pl.pallas_call(lambda *refs: kernel(rows_n, cols_n, panels, width, *refs)...  51.9 us
    unnamed x2, local copies, waits for them, and re-layouts  1.27 us

profile of v3, /device:TPU:33, one launch (start us, length us, event | category | flops | bytes accessed | tf_op | source)
XLA Modules:
  0.0 53.8 jit_solution(10593161234891083043)
XLA Ops:
  0.6 51.9 %solve.1 = (bf16[4,16,256]{2,1,0:T(8,128)(2,1)S(1)}, bf16[256,256]{1,0:T(8,128)(2,1)S(1)}) custom-call(bf16[4,16,4096]{2,1,0:T(8,128)(2,1)} %refs_0_.1, s32[4,16]{1,0:T(4,128)} %bitcast.1, bf16[4,16,256]{2,1,0:T(8,128)(2,1)} %refs_2_.1, bf16[256,256]{1,0:T(8,128)(2,1)} %refs_3_.1, bf16[256,256]{1,0:T(8,128)(2,1)} %refs_4_.1), custom_call_target="tpu_custom_call" | custom-call | tf_op jit(solution)/shard_map/solve/pallas_call | solution.py:497
  52.6 0.6 %copy.9 = bf16[4,16,256]{2,1,0:T(8,128)(2,1)} copy(bf16[4,16,256]{2,1,0:T(8,128)(2,1)S(1)} %get-tuple-element.4) | data formatting | bytes 65536
  53.2 0.7 %copy.10 = bf16[256,256]{1,0:T(8,128)(2,1)} copy(bf16[256,256]{1,0:T(8,128)(2,1)S(1)} %get-tuple-element.5) | data formatting | bytes 262144

commit v4 on v3

--- a/solution.py
+++ b/solution.py
@@ -7,7 +7,7 @@
 from jax.experimental.pallas import tpu as pltpu
 from jax.sharding import PartitionSpec as P
 
-ROOT = 0
+ROOT = 1
 F32 = jnp.float32
 BF16 = jnp.bfloat16
 
@@ -70,11 +70,14 @@
     def _():
         lax.fori_loop(1, rows_n, greet_row, 0)
 
-    @pl.when(lax.rem(row, 2) == 1)
-    def _():
-        signal(barrier, prow=row - 1)
-
-    expected = cols_n - 1 + jnp.where(is_root, 0, 1) + (1 - lax.rem(row, 2))
+    beside = row + 1 - 2 * lax.rem(row, 2)
+    same_core = lax.rem(row, 2) == ROOT % 2
+
+    @pl.when(lax.rem(row, 2) != ROOT % 2)
+    def _():
+        signal(barrier, prow=beside)
+
+    expected = cols_n - 1 + jnp.where(is_root, 0, 1) + jnp.where(same_core, 1, 0)
     pl.semaphore_wait(barrier, expected)
 
     def strip(ref, j):
@@ -109,8 +112,11 @@
             self.each("wait_send")
 
     def any_peer(i):
-        j = lax.rem(col + i, cols_n)
-        return j, j
+        at = lax.rem(i + cols_n // 2 + side // 2 - 1, cols_n)
+        at = jnp.where(at < cols_n // 2 + side // 2 - 1, at + 1, at)
+        jx = lax.rem(x + lax.div(at, side), side)
+        jy = lax.rem(y + lax.rem(at, side), side)
+        return jx * side + jy, jx * side + jy
 
     def x_peer(i):
         j = lax.rem(x + i, side)
@@ -145,19 +151,6 @@
     )
     sol_x = over_all(lambda j: strip(spread, j), lambda j: sol_in.at[j], ta, tb)
 
-    factor_x.start()
-    later_x.start()
-    own_copies = [
-        pltpu.make_async_copy(factor_quarter(x), strip(part, x), loc.at[1]),
-        pltpu.make_async_copy(later, later_strip(y), loc.at[2]),
-    ]
-    for copy in own_copies:
-        copy.start()
-
-    @pl.when(row != ROOT)
-    def _():
-        signal(hello, prow=ROOT)
-
     def lead_copy(q):
         first = q * (q - 1) // 2
         return remote(
@@ -168,16 +161,37 @@
             prow=ROOT,
         )
 
+    def lead_here():
+        first = ROOT * (ROOT - 1) // 2
+        return pltpu.make_async_copy(
+            factor.at[pl.ds(0, ROOT), :, pl.ds(0, width)],
+            lead_own.at[pl.ds(first, ROOT)],
+            loc.at[6],
+        )
+
     for q in range(1, panels):
 
         @pl.when(row == q)
         def _(q=q):
-            lead_copy(q).start()
+            (lead_here() if q == ROOT else lead_copy(q)).start()
 
     @pl.when(is_root)
     def _():
         inv_x.start()
         pltpu.make_async_copy(diag, strip(inv, turned(col)), loc.at[3]).start()
+
+    factor_x.start()
+    later_x.start()
+    own_copies = [
+        pltpu.make_async_copy(factor_quarter(x), strip(part, x), loc.at[1]),
+        pltpu.make_async_copy(later, later_strip(y), loc.at[2]),
+    ]
+    for copy in own_copies:
+        copy.start()
+
+    @pl.when(row != ROOT)
+    def _():
+        signal(hello, prow=ROOT)
 
     fetch.wait()
     fetch_pattern.wait()
@@ -204,7 +218,8 @@
     def rt_send(q):
         return remote(rt_own, rt_all.at[q], qa, qb.at[q], prow=ROOT)
 
-    for q in range(1, panels):
+    others = [q for q in range(panels) if q != ROOT]
+    for q in others:
 
         @pl.when(row == q)
         def _(q=q):
@@ -212,9 +227,13 @@
 
     @pl.when(is_root)
     def _():
-        rt_all[0] = rt_own[...]
+        rt_all[ROOT] = rt_own[...]
         for q in range(1, panels):
-            lead_copy(q).wait_recv()
+            if q == ROOT:
+                lead_here().wait()
+            else:
+                lead_copy(q).wait_recv()
+
         lead_x.start()
         pltpu.make_async_copy(lead_own, strip(lead, turned(col)), loc.at[4]).start()
 
@@ -253,14 +272,13 @@
 
     def along_row(send):
         def step(i, _):
-            send(2 * i).start()
+            send(lax.rem(ROOT + 2 * i, rows_n)).start()
             return 0
 
         lax.fori_loop(1, chips, step, 0)
-        send(1).start()
-
-    first_core = lax.rem(row, 2) == 0
-    relays = first_core & (row != ROOT)
+        send(beside).start()
+
+    relays = same_core & (row != ROOT)
 
     def y_send(r):
         return remote(y_own, y_own, ya.at[r], yb, prow=r)
@@ -273,7 +291,7 @@
         pltpu.make_async_copy(lead_own, strip(lead, turned(col)), loc.at[4]).wait()
         solved = []
         for q in range(panels):
-            if q > 0:
+            if q != ROOT:
                 rt_send(q).wait_recv()
             residual = rt_all[q].astype(F32)
             for p in range(q):
@@ -284,10 +302,9 @@
         for j in range(side):
             pieces = [y_q[:, j * group : (j + 1) * group] for y_q in solved]
             y_own[j] = jnp.concatenate(pieces, axis=1)
+        y_x.start()
         pl.semaphore_wait(hello, rows_n - 1)
-
         along_row(y_send)
-        y_x.start()
 
     bulk_x.arrive()
     def sum_step(i, sums):
@@ -306,13 +323,25 @@
     @pl.when(row != ROOT)
     def _():
         z_send(row).start()
-        y_send(0).wait_recv()
+        y_send(ROOT).wait_recv()
 
         @pl.when(relays)
         def _():
-            y_send(row + 1).start()
+            y_send(beside).start()
 
         y_x.start()
+
+    y_all[col] = y_own[y]
+    y_x.arrive()
+
+    def lower_step(j, _):
+        strip_j = part[:, :, block_of(j)].reshape(columns, width)
+        low[j] = dot(y_all[...].reshape(-1, columns), strip_j).astype(BF16)
+        return 0
+
+    lax.fori_loop(0, side, lower_step, 0)
+    low_x.start()
+    low_in[y] = low[y]
 
     def out_send(r):
         return remote(out_buf, out_buf, oa.at[r], ob, prow=r)
@@ -320,8 +349,9 @@
     @pl.when(is_root)
     def _():
         def gather_step(r, sums):
-            z_send(r).wait_recv()
-            return tuple(t + z_in[r, p].astype(F32) for p, t in enumerate(sums))
+            sender = lax.rem(ROOT + r, rows_n)
+            z_send(sender).wait_recv()
+            return tuple(t + z_in[sender, p].astype(F32) for p, t in enumerate(sums))
 
         gathered = lax.fori_loop(
             1, rows_n, gather_step, tuple(z_own[p].astype(F32) for p in range(panels))
@@ -348,18 +378,6 @@
         mine = pl.ds(pl.multiple_of(col * narrow, narrow), narrow)
         sol_in[col] = spread[:, mine, :]
 
-    y_all[col] = y_own[y]
-    y_x.arrive()
-
-    def lower_step(j, _):
-        strip_j = part[:, :, block_of(j)].reshape(columns, width)
-        low[j] = dot(y_all[...].reshape(-1, columns), strip_j).astype(BF16)
-        return 0
-
-    lax.fori_loop(0, side, lower_step, 0)
-    low_x.start()
-    low_in[y] = low[y]
-
     @pl.when(is_root)
     def _():
         sol_x.arrive()
@@ -385,11 +403,11 @@
 
     @pl.when(row != ROOT)
     def _():
-        out_send(0).wait_recv()
+        out_send(ROOT).wait_recv()
 
         @pl.when(relays)
         def _():
-            out_send(row + 1).start()
+            out_send(beside).start()
 
     sol_out[...] = out_buf[...]
 
@@ -404,11 +422,12 @@
 
         lax.fori_loop(1, cols_n, step, 0)
 
-    for q in range(1, panels):
+    for q in others:
 
         @pl.when(row == q)
         def _(q=q):
-            lead_copy(q).wait_send()
+            if q > 0:
+                lead_copy(q).wait_send()
             rt_send(q).wait_send()
 
     @pl.when(row != ROOT)
@@ -422,16 +441,17 @@
         sol_x.drain()
 
         def step(i, _):
-            y_send(2 * i).wait_send()
-            out_send(2 * i).wait_send()
+            to = lax.rem(ROOT + 2 * i, rows_n)
+            y_send(to).wait_send()
+            out_send(to).wait_send()
             return 0
 
         lax.fori_loop(1, chips, step, 0)
 
-    @pl.when(first_core)
-    def _():
-        y_send(row + 1).wait_send()
-        out_send(row + 1).wait_send()
+    @pl.when(same_core)
+    def _():
+        y_send(beside).wait_send()
+        out_send(beside).wait_send()
 
 
 def solution(mesh):

time: 54 us -> 51.6 us (0.956)
  the two profiles are of different devices: /device:TPU:33 before, /device:TPU:1 now
where the time goes in v4:
time: 51.6 us; the launch traced here: 51.4 us
  Pallas kernels  49.5 us (96%)
  local copies, waits for them, and re-layouts  1.27 us (2%)
  between operations  0.64 us (1%)
    pallas_call x1, Pallas kernels, on_device(): pl.pallas_call(lambda *refs: kernel(rows_n, cols_n, panels, width, *refs)...  49.5 us
    unnamed x2, local copies, waits for them, and re-layouts  1.27 us

profile of v4, /device:TPU:1, one launch (start us, length us, event | category | flops | bytes accessed | tf_op | source)
XLA Modules:
  0.0 51.4 jit_solution(15693132685533754699)
XLA Ops:
  0.6 49.5 %solve.1 = (bf16[4,16,256]{2,1,0:T(8,128)(2,1)S(1)}, bf16[256,256]{1,0:T(8,128)(2,1)S(1)}) custom-call(bf16[4,16,4096]{2,1,0:T(8,128)(2,1)} %refs_0_.1, s32[4,16]{1,0:T(4,128)} %bitcast.1, bf16[4,16,256]{2,1,0:T(8,128)(2,1)} %refs_2_.1, bf16[256,256]{1,0:T(8,128)(2,1)} %refs_3_.1, bf16[256,256]{1,0:T(8,128)(2,1)} %refs_4_.1), custom_call_target="tpu_custom_call" | custom-call | tf_op jit(solution)/shard_map/solve/pallas_call | solution.py:517
  50.2 0.6 %copy.9 = bf16[4,16,256]{2,1,0:T(8,128)(2,1)} copy(bf16[4,16,256]{2,1,0:T(8,128)(2,1)S(1)} %get-tuple-element.4) | data formatting | bytes 65536
  50.8 0.7 %copy.10 = bf16[256,256]{1,0:T(8,128)(2,1)} copy(bf16[256,256]{1,0:T(8,128)(2,1)S(1)} %get-tuple-element.5) | data formatting | bytes 262144

commit v5 on v4

--- a/solution.py
+++ b/solution.py
@@ -334,13 +334,18 @@
     y_all[col] = y_own[y]
     y_x.arrive()
 
-    def lower_step(j, _):
+    def lower_strip(j):
         strip_j = part[:, :, block_of(j)].reshape(columns, width)
         low[j] = dot(y_all[...].reshape(-1, columns), strip_j).astype(BF16)
+
+    def lower_step(i, _):
+        device, j = y_peer(i)
+        lower_strip(j)
+        remote(low.at[j], low_in.at[y], wa.at[i], wb.at[y], pcol=device).start()
         return 0
 
-    lax.fori_loop(0, side, lower_step, 0)
-    low_x.start()
+    lax.fori_loop(1, side, lower_step, 0)
+    lower_strip(y)
     low_in[y] = low[y]
 
     def out_send(r):

time: 51.6 us -> 51.6 us (level)
  no operation moved by 1% of the time
where the time goes in v5:
time: 51.6 us; the launch traced here: 51.4 us
  Pallas kernels  49.5 us (96%)
  local copies, waits for them, and re-layouts  1.27 us (2%)
  between operations  0.64 us (1%)
    pallas_call x1, Pallas kernels, on_device(): pl.pallas_call(lambda *refs: kernel(rows_n, cols_n, panels, width, *refs)...  49.5 us
    unnamed x2, local copies, waits for them, and re-layouts  1.27 us

profile of v5, /device:TPU:1, one launch (start us, length us, event | category | flops | bytes accessed | tf_op | source)
XLA Modules:
  0.0 51.4 jit_solution(16965877715918807089)
XLA Ops:
  0.6 49.5 %solve.1 = (bf16[4,16,256]{2,1,0:T(8,128)(2,1)S(1)}, bf16[256,256]{1,0:T(8,128)(2,1)S(1)}) custom-call(bf16[4,16,4096]{2,1,0:T(8,128)(2,1)} %refs_0_.1, s32[4,16]{1,0:T(4,128)} %bitcast.1, bf16[4,16,256]{2,1,0:T(8,128)(2,1)} %refs_2_.1, bf16[256,256]{1,0:T(8,128)(2,1)} %refs_3_.1, bf16[256,256]{1,0:T(8,128)(2,1)} %refs_4_.1), custom_call_target="tpu_custom_call" | custom-call | tf_op jit(solution)/shard_map/solve/pallas_call | solution.py:522
  50.2 0.6 %copy.9 = bf16[4,16,256]{2,1,0:T(8,128)(2,1)} copy(bf16[4,16,256]{2,1,0:T(8,128)(2,1)S(1)} %get-tuple-element.4) | data formatting | bytes 65536
  50.8 0.7 %copy.10 = bf16[256,256]{1,0:T(8,128)(2,1)} copy(bf16[256,256]{1,0:T(8,128)(2,1)S(1)} %get-tuple-element.5) | data formatting | bytes 262144
